TPU v7x, 256 devices: a whole 4x4x8 slice. The times are simulated.
256 devices in a mesh: rows: 32 (over z, y), cols: 8 (over x, core).
Axes of the slice: x: 4, y: 4, z: 8, core: 2. Of those that a mesh axis runs over, the one named last changes fastest.
Arguments:
- matrix: float32 [32768, 10, 1024], P('rows', None, 'cols'), may hold values from -6 to 6
Outputs:
- reduced: float32 [32768, 10, 1024], P('rows', None, 'cols')
- top_rows: float32 [256, 10, 1024], P(None, None, 'cols')
All inputs are finite; a program needn't handle non-finite values.
Results may differ from a plain program's by a relative error of at most 0.0001.
Values sent between devices are 32-bit elements; how exact they have to be, the bound alone decides.
No kernel may reach another device: no remote copies, remote signals or barrier semaphores. Data moves between devices by JAX's collectives and lax.ppermute only.
A program may use at most 64 MiB of HBM per device.

v0:
```python
import jax
import jax.numpy as jnp
from jax import lax
from jax.sharding import PartitionSpec as P

PRECISE = lax.Precision.HIGHEST


def spread(block, axis, owner):
    block = jnp.where(lax.axis_index(axis) == owner, block, jnp.zeros_like(block))
    return lax.psum(block, axis)


def product(left, right):
    return jnp.dot(left, right, precision=PRECISE, preferred_element_type=jnp.float32)


def relay_panel(panel_block, root_index):
    return spread(panel_block, "cols", root_index)


def factor(panel, columns):
    gram_block = product(panel.T, panel)
    cross_terms = product(panel.T, columns)
    gram_block, cross_terms = lax.psum((gram_block, cross_terms), "rows")
    triangle = jnp.linalg.cholesky(gram_block)
    weights = jax.scipy.linalg.solve_triangular(triangle, cross_terms, lower=True)
    coefficients = jax.scipy.linalg.solve_triangular(triangle, weights, trans=1, lower=True)
    return (weights, columns - product(panel, coefficients))


def shards(matrix):
    rows_dev, rounds, width = matrix.shape
    columns = matrix.reshape(rows_dev, rounds * width)
    first_panel = relay_panel(columns[:, :width], 0)
    first_rows, columns = factor(first_panel, columns)
    second_panel = relay_panel(columns[:, :width], 1)
    second_rows, columns = factor(second_panel, columns)
    triangle_rows = jnp.concatenate([first_rows, second_rows], axis=0)
    return (
        columns.reshape(rows_dev, rounds, width),
        triangle_rows.reshape(2 * width, rounds, width),
    )


def solution(mesh):
    placed = (P("rows", None, "cols"),)
    return jax.shard_map(
        shards,
        mesh=mesh,
        in_specs=placed,
        out_specs=(P("rows", None, "cols"), P(None, None, "cols")),
        check_vma=False,
    )
```

profile of v0, /device:TPU:2, one launch (start us, length us, event | category | flops | bytes accessed | tf_op | source)
XLA Modules:
  0.0 562.0 jit_solution(4598258446387686267)
XLA Ops:
  7.2 5.9 %copy.10 = f32[1024,10,128]{0,2,1:T(8,128)} copy(f32[1024,10,128]{2,0,1:T(8,128)} %param.6) | data formatting | bytes 10485760 | tf_op args[0]
  13.1 5.9 %copy.14 = f32[1024,1280]{1,0:T(8,128)} copy(f32[1024,1280]{0,1:T(8,128)} %bitcast.45) | data formatting | bytes 10485760 | tf_op jit(solution)/shard_map/reshape | solution.py:34
  19.0 1.9 slice_select_fusion.1
  21.0 66.6 %all-reduce.7.cloned.1.call-done = f32[1024,128]{1,0:T(8,128)} async-done(((f32[1024,128]{1,0:T(8,128)}), f32[1024,128]{1,0:T(8,128)}) %all-reduce.7.cloned.1.call-update) | async-done | bytes 524304 | tf_op jit(solution)/shard_map/psum | solution.py:11
  87.6 8.0 %fusion.13 = f32[128,1280]{1,0:T(8,128)} fusion(f32[1024,128]{1,0:T(8,128)} %all-reduce.7.cloned.1.call-done, f32[1024,1280]{0,1:T(8,128)} %bitcast.46), kind=kOutput, calls=%fused_computation.28 | convolution fusion | flops 2013265920 | bytes 6422528 | tf_op jit(solution)/shard_map/dot_general | solution.py:15
  95.5 1.6 fusion.12
  97.4 150.1 %all-reduce.13.cloned.1.call-done = (f32[128,1280]{1,0:T(8,128)}, f32[128,128]{0,1:T(8,128)}) async-done(((f32[128,1280]{1,0:T(8,128)}, f32[128,128]{0,1:T(8,128)}), (f32[128,1280]{1,0:T(8,128)}, f32[128,128]{0,1:T(8,128)})) %all-reduce.13.cloned.1.call-update) | async-done | bytes 720912 | tf_op jit(solution)/shard_map/psum | solution.py:25
  247.5 0.9 copy.13
  248.5 0.9 fusion.11
  249.3 11.7 %cholesky.44 = f32[128,128]{1,0:T(8,128)S(1)} custom-call(f32[128,128]{1,0:T(8,128)S(1)} %fusion.11), custom_call_target="Cholesky" | custom-call | tf_op jit(solution)/shard_map/jit(cholesky)/cholesky | solution.py:26
  261.7 0.7 fusion
  262.4 9.8 %custom-call.11 = f32[1,128,128]{1,2,0:T(8,128)S(1)} custom-call(f32[1,128,128]{2,1,0:T(8,128)S(1)} %fusion), custom_call_target="InvertDiagBlocksLowerTriangular" | custom-call | tf_op jit(solution)/shard_map/jit(_solve_triangular)/triangular_solve | solution.py:28
  272.2 1.8 fusion.7
  274.0 0.7 fusion.9
  274.7 6.4 %convolution_subtract_fusion.1 = f32[1024,1280]{1,0:T(8,128)S(1)} fusion(f32[1024,1280]{1,0:T(8,128)} %copy.14, f32[1024,128]{1,0:T(8,128)S(1)} %copy-done.1, f32[128,1280]{1,0:T(8,128)S(1)} %fusion.9), kind=kOutput, calls=%fused_computation.1 | convolution fusion | flops 2014576640 | bytes 11665408 | tf_op jit(solution)/shard_map/dot_general | solution.py:15
  281.1 2.3 copy-done
  283.4 0.8 slice_select_fusion
  284.6 60.2 %all-reduce.9.cloned.1.call-done = f32[1024,128]{1,0:T(8,128)} async-done(((f32[1024,128]{1,0:T(8,128)}), f32[1024,128]{1,0:T(8,128)}) %all-reduce.9.cloned.1.call-update) | async-done | bytes 524304 | tf_op jit(solution)/shard_map/psum | solution.py:11
  344.8 2.9 fusion.14
  347.6 6.3 %fusion.15 = f32[128,1280]{1,0:T(8,128)} fusion(f32[1024,128]{1,0:T(8,128)} %all-reduce.9.cloned.1.call-done, f32[1024,1280]{1,0:T(8,128)} %copy-done), kind=kOutput, calls=%fused_computation.30 | convolution fusion | flops 2013265920 | bytes 6422528 | tf_op jit(solution)/shard_map/dot_general | solution.py:15
  354.0 150.2 %all-reduce.11.cloned.1.call-done = (f32[128,1280]{1,0:T(8,128)}, f32[128,128]{0,1:T(8,128)}) async-done(((f32[128,1280]{1,0:T(8,128)}, f32[128,128]{0,1:T(8,128)}), (f32[128,1280]{1,0:T(8,128)}, f32[128,128]{0,1:T(8,128)})) %all-reduce.11.cloned.1.call-update) | async-done | bytes 720912 | tf_op jit(solution)/shard_map/psum | solution.py:25
  504.2 0.9 copy.16
  505.2 0.9 fusion.6
  506.0 11.7 %cholesky.55 = f32[128,128]{1,0:T(8,128)S(1)} custom-call(f32[128,128]{1,0:T(8,128)S(1)} %fusion.6), custom_call_target="Cholesky" | custom-call | tf_op jit(solution)/shard_map/jit(cholesky)/cholesky | solution.py:26
  519.1 9.8 %custom-call.13 = f32[1,128,128]{1,2,0:T(8,128)S(1)} custom-call(f32[1,128,128]{2,1,0:T(8,128)S(1)} %fusion.1), custom_call_target="InvertDiagBlocksLowerTriangular" | custom-call | tf_op jit(solution)/shard_map/jit(_solve_triangular)/triangular_solve | solution.py:28
  528.9 1.8 fusion.2
  530.7 0.7 fusion.4
  531.5 7.9 %convolution_subtract_fusion = f32[1024,1280]{1,0:T(8,128)} fusion(f32[1024,1280]{1,0:T(8,128)} %copy-done, f32[1024,128]{1,0:T(8,128)S(1)} %copy-done.2, f32[128,1280]{1,0:T(8,128)S(1)} %fusion.4), kind=kOutput, calls=%fused_computation | convolution fusion | flops 2014576640 | bytes 11665408 | tf_op jit(solution)/shard_map/dot_general | solution.py:15
  539.4 5.9 %copy.17 = f32[1024,1280]{0,1:T(8,128)} copy(f32[1024,1280]{1,0:T(8,128)} %convolution_subtract_fusion) | data formatting | bytes 10485760 | tf_op jit(solution)/shard_map/sub | solution.py:29
  545.4 5.9 %copy.19 = f32[1024,10,128]{2,0,1:T(8,128)} copy(f32[1024,10,128]{0,2,1:T(8,128)} %bitcast.47) | data formatting | bytes 10485760
  551.2 1.5 copy.18
  552.7 2.8 copy.20
  (19 shorter events, 2.7 us)
Async XLA Ops:
  7.2 80.4 %all-reduce.7.cloned.1.call-start = ((), (), s32[]{:S(2)}) async-start(), calls=%async_computation | async-start | bytes 1048576 | tf_op jit(solution)/shard_map/psum | solution.py:11
  20.9 226.6 %all-reduce.13.cloned.1.call-start = ((), (), s32[]{:S(2)}) async-start(), calls=%async_computation.3 | async-start | bytes 1441792 | tf_op jit(solution)/shard_map/psum | solution.py:25
  87.6 8.0 %copy-start.1 = (f32[1024,128]{1,0:T(8,128)S(1)}, f32[1024,128]{1,0:T(8,128)}, u32[]{:S(2)}) copy-start(f32[1024,128]{1,0:T(8,128)} %all-reduce.7.cloned.1.call-done) | copy-start | bytes 1572868
  97.2 247.6 %all-reduce.9.cloned.1.call-start = ((), (), s32[]{:S(2)}) async-start(), calls=%async_computation.1 | async-start | bytes 1048576 | tf_op jit(solution)/shard_map/psum | solution.py:11
  281.1 2.4 copy-start
  284.3 220.0 %all-reduce.11.cloned.1.call-start = ((), (), s32[]{:S(2)}) async-start(), calls=%async_computation.2 | async-start | bytes 1441792 | tf_op jit(solution)/shard_map/psum | solution.py:25
  347.6 183.9 %copy-start.2 = (f32[1024,128]{1,0:T(8,128)S(1)}, f32[1024,128]{1,0:T(8,128)}, u32[]{:S(2)}) copy-start(f32[1024,128]{1,0:T(8,128)} %all-reduce.9.cloned.1.call-done) | copy-start | bytes 1572868
Sparse Core Ops, SparseCore 0:
  21.1 66.4 all-reduce.6
  97.3 150.1 all-reduce.12
  284.4 60.3 all-reduce.8
  354.1 150.0 all-reduce.10
where the time goes:
time: 563 us; the launch traced here: 562 us
  waiting for transfers between devices  427 us (76%)
  other arithmetic  50.2 us (9%)
  matrix products  38.1 us (7%)
  local copies, waits for them, and re-layouts  32.1 us (6%)
  between operations  13.9 us (2%)
    psum x2, waiting for transfers between devices, factor(): gram_block, cross_terms = lax.psum((gram_block, cross_terms), 'rows')  300 us
    psum x2, waiting for transfers between devices, spread(): return lax.psum(block, axis)  127 us
    dot_general x6, matrix products, product(): jnp.dot(left, right, precision=PRECISE, preferred_element_type=jnp.float32)  33.1 us
    another operation x6, other arithmetic, factor(): triangle = jnp.linalg.cholesky(gram_block)  24.8 us
    another operation x4, other arithmetic, factor(): jax.scipy.linalg.solve_triangular(triangle, weights, trans=1, lower=True)  20.9 us
    unnamed x9, local copies, waits for them, and re-layouts  16.9 us
  transfers between devices with their start and end apart: 4, of which 4 were waited for; matrix products, arithmetic and copies ran while one was open for 0% of the time, Pallas kernels for 0%

commit v1 on v0

--- a/solution.py
+++ b/solution.py
@@ -4,11 +4,12 @@
 from jax.sharding import PartitionSpec as P
 
 PRECISE = lax.Precision.HIGHEST
+process_desk_over_axis = lambda mine_x, row_axis: lax.all_gather(mine_x, row_axis).sum(axis=0)
 
 
 def spread(block, axis, owner):
     block = jnp.where(lax.axis_index(axis) == owner, block, jnp.zeros_like(block))
-    return lax.psum(block, axis)
+    return process_desk_over_axis(block, axis)
 
 
 def product(left, right):

time: 563 us -> 506 us (0.90)
  waiting for transfers between devices: 427 us -> 366 us
    psum x2 -> x0, waiting for transfers between devices: 127 us -> none  [spread(): return lax.psum(block, axis)]
    all_gather x0 -> x2, waiting for transfers between devices: none -> 66.9 us  [lax.all_gather(mine_x, row_axis).sum(axis=0)]
    unnamed x9 -> x5, local copies, waits for them, and re-layouts: 16.9 us -> 16.9 us
where the time goes in v1:
time: 506 us; the launch traced here: 505 us
  waiting for transfers between devices  366 us (72%)
  other arithmetic  55.1 us (11%)
  matrix products  36.4 us (7%)
  local copies, waits for them, and re-layouts  32.1 us (6%)
  between operations  13.9 us (3%)
    psum x2, waiting for transfers between devices, factor(): gram_block, cross_terms = lax.psum((gram_block, cross_terms), 'rows')  299 us
    all_gather x2, waiting for transfers between devices, lax.all_gather(mine_x, row_axis).sum(axis=0)  66.9 us
    dot_general x6, matrix products, product(): jnp.dot(left, right, precision=PRECISE, preferred_element_type=jnp.float32)  31.5 us
    another operation x6, other arithmetic, factor(): triangle = jnp.linalg.cholesky(gram_block)  24.8 us
    another operation x4, other arithmetic, factor(): jax.scipy.linalg.solve_triangular(triangle, weights, trans=1, lower=True)  20.9 us
    unnamed x5, local copies, waits for them, and re-layouts  16.9 us
  transfers between devices with their start and end apart: 4, of which 4 were waited for; matrix products, arithmetic and copies ran while one was open for 0% of the time, Pallas kernels for 0%

profile of v1, /device:TPU:2, one launch (start us, length us, event | category | flops | bytes accessed | tf_op | source)
XLA Modules:
  0.0 504.5 jit_solution(17908171459436652079)
XLA Ops:
  7.2 5.9 %copy.10 = f32[1024,10,128]{0,2,1:T(8,128)} copy(f32[1024,10,128]{2,0,1:T(8,128)} %param.6) | data formatting | bytes 10485760 | tf_op args[0]
  13.1 5.9 %copy.14 = f32[1024,1280]{1,0:T(8,128)} copy(f32[1024,1280]{0,1:T(8,128)} %bitcast.47) | data formatting | bytes 10485760 | tf_op jit(solution)/shard_map/reshape | solution.py:35
  19.0 1.9 slice_select_fusion.1
  21.0 36.7 %all-gather.5.cloned.1.call-done = f32[8192,128]{1,0:T(8,128)} async-done(((f32[1024,128]{1,0:T(8,128)}), f32[8192,128]{1,0:T(8,128)}) %all-gather.5.cloned.1.call-update) | async-done | bytes 4194320 | tf_op jit(solution)/shard_map/all_gather | solution.py:7
  57.7 2.4 reduce_sum.18
  60.1 7.8 %fusion.13 = f32[128,1280]{1,0:T(8,128)} fusion(f32[1024,128]{1,0:T(8,128)S(1)} %reduce_sum.18, f32[1024,1280]{0,1:T(8,128)} %bitcast.48), kind=kOutput, calls=%fused_computation.28 | convolution fusion | flops 2013265920 | bytes 6422528 | tf_op jit(solution)/shard_map/dot_general | solution.py:16
  67.9 1.6 fusion.12
  69.8 149.7 %all-reduce.7.cloned.1.call-done = (f32[128,1280]{1,0:T(8,128)}, f32[128,128]{0,1:T(8,128)}) async-done(((f32[128,1280]{1,0:T(8,128)}, f32[128,128]{0,1:T(8,128)}), (f32[128,1280]{1,0:T(8,128)}, f32[128,128]{0,1:T(8,128)})) %all-reduce.7.cloned.1.call-update) | async-done | bytes 720912 | tf_op jit(solution)/shard_map/psum | solution.py:26
  219.4 0.9 copy.13
  220.4 0.9 fusion.11
  221.2 11.7 %cholesky.44 = f32[128,128]{1,0:T(8,128)S(1)} custom-call(f32[128,128]{1,0:T(8,128)S(1)} %fusion.11), custom_call_target="Cholesky" | custom-call | tf_op jit(solution)/shard_map/jit(cholesky)/cholesky | solution.py:27
  234.3 9.8 %custom-call.11 = f32[1,128,128]{1,2,0:T(8,128)S(1)} custom-call(f32[1,128,128]{2,1,0:T(8,128)S(1)} %fusion), custom_call_target="InvertDiagBlocksLowerTriangular" | custom-call | tf_op jit(solution)/shard_map/jit(_solve_triangular)/triangular_solve | solution.py:29
  244.1 1.8 fusion.7
  245.9 0.7 fusion.9
  246.6 6.4 %convolution_subtract_fusion.1 = f32[1024,1280]{1,0:T(8,128)S(1)} fusion(f32[1024,1280]{1,0:T(8,128)} %copy.14, f32[1024,128]{1,0:T(8,128)S(1)} %reduce_sum.18, f32[128,1280]{1,0:T(8,128)S(1)} %fusion.9), kind=kOutput, calls=%fused_computation.1 | convolution fusion | flops 2014576640 | bytes 11665408 | tf_op jit(solution)/shard_map/dot_general | solution.py:16
  253.0 2.3 copy-done
  255.4 0.8 slice_select_fusion
  256.5 30.2 %all-gather.7.cloned.1.call-done = f32[8192,128]{1,0:T(8,128)} async-done(((f32[1024,128]{1,0:T(8,128)}), f32[8192,128]{1,0:T(8,128)}) %all-gather.7.cloned.1.call-update) | async-done | bytes 4194320 | tf_op jit(solution)/shard_map/all_gather | solution.py:7
  286.7 2.4 reduce_sum.19
  289.2 1.6 fusion.14
  290.8 6.1 %fusion.15 = f32[128,1280]{1,0:T(8,128)} fusion(f32[1024,128]{1,0:T(8,128)S(1)} %reduce_sum.19, f32[1024,1280]{1,0:T(8,128)} %copy-done), kind=kOutput, calls=%fused_computation.30 | convolution fusion | flops 2013265920 | bytes 6422528 | tf_op jit(solution)/shard_map/dot_general | solution.py:16
  296.9 149.8 %all-reduce.5.cloned.1.call-done = (f32[128,1280]{1,0:T(8,128)}, f32[128,128]{0,1:T(8,128)}) async-done(((f32[128,1280]{1,0:T(8,128)}, f32[128,128]{0,1:T(8,128)}), (f32[128,1280]{1,0:T(8,128)}, f32[128,128]{0,1:T(8,128)})) %all-reduce.5.cloned.1.call-update) | async-done | bytes 720912 | tf_op jit(solution)/shard_map/psum | solution.py:26
  446.7 0.9 copy.16
  447.7 0.9 fusion.6
  448.5 11.7 %cholesky.55 = f32[128,128]{1,0:T(8,128)S(1)} custom-call(f32[128,128]{1,0:T(8,128)S(1)} %fusion.6), custom_call_target="Cholesky" | custom-call | tf_op jit(solution)/shard_map/jit(cholesky)/cholesky | solution.py:27
  461.6 9.8 %custom-call.13 = f32[1,128,128]{1,2,0:T(8,128)S(1)} custom-call(f32[1,128,128]{2,1,0:T(8,128)S(1)} %fusion.1), custom_call_target="InvertDiagBlocksLowerTriangular" | custom-call | tf_op jit(solution)/shard_map/jit(_solve_triangular)/triangular_solve | solution.py:29
  471.4 1.8 fusion.2
  474.0 7.9 %convolution_subtract_fusion = f32[1024,1280]{1,0:T(8,128)} fusion(f32[1024,1280]{1,0:T(8,128)} %copy-done, f32[1024,128]{1,0:T(8,128)S(1)} %reduce_sum.19, f32[128,1280]{1,0:T(8,128)S(1)} %fusion.4), kind=kOutput, calls=%fused_computation | convolution fusion | flops 2014576640 | bytes 11665408 | tf_op jit(solution)/shard_map/dot_general | solution.py:16
  481.9 5.9 %copy.17 = f32[1024,1280]{0,1:T(8,128)} copy(f32[1024,1280]{1,0:T(8,128)} %convolution_subtract_fusion) | data formatting | bytes 10485760 | tf_op jit(solution)/shard_map/sub | solution.py:30
  487.9 5.9 %copy.19 = f32[1024,10,128]{2,0,1:T(8,128)} copy(f32[1024,10,128]{0,2,1:T(8,128)} %bitcast.49) | data formatting | bytes 10485760
  493.7 1.5 copy.18
  495.2 2.8 copy.20
  (17 shorter events, 4.1 us)
Async XLA Ops:
  7.2 50.5 %all-gather.5.cloned.1.call-start = ((), (), s32[]{:S(2)}) async-start(), calls=%async_computation | async-start | bytes 4718592 | tf_op jit(solution)/shard_map/all_gather | solution.py:7
  20.9 198.5 %all-reduce.7.cloned.1.call-start = ((), (), s32[]{:S(2)}) async-start(), calls=%async_computation.3 | async-start | bytes 1441792 | tf_op jit(solution)/shard_map/psum | solution.py:26
  69.5 217.2 %all-gather.7.cloned.1.call-start = ((), (), s32[]{:S(2)}) async-start(), calls=%async_computation.1 | async-start | bytes 4718592 | tf_op jit(solution)/shard_map/all_gather | solution.py:7
  253.0 2.4 copy-start
  256.2 190.5 %all-reduce.5.cloned.1.call-start = ((), (), s32[]{:S(2)}) async-start(), calls=%async_computation.2 | async-start | bytes 1441792 | tf_op jit(solution)/shard_map/psum | solution.py:26
Sparse Core Ops, SparseCore 0:
  21.1 36.5 all-gather.4
  69.7 149.7 all-reduce.6
  256.3 30.3 all-gather.6
  297.1 149.6 all-reduce.4
